TPU v7x, 32 devices: a whole 2x2x4 slice. The times are simulated.
32 devices in a mesh: roll: 16 (over z, y, core), tensor: 2 (over x).
Axes of the slice: x: 2, y: 2, z: 4, core: 2. Of those that a mesh axis runs over, the one named last changes fastest.
Arguments:
- grad_out: bfloat16 [6144, 5120], P('roll', 'tensor'), may hold values from -6 to 6
- out_weight: bfloat16 [5120, 4096], P('roll', 'tensor'), may hold values from -0.078125 to 0.078125
- queries: bfloat16 [6144, 4096], P('roll', 'tensor'), may hold values from -6 to 6
- resp_key: bfloat16 [6144, 1024], P('roll', 'tensor'), may hold values from -5 to 5
- resp_value: bfloat16 [6144, 1024], P('roll', 'tensor'), may hold values from -5 to 5
- prefix_key: bfloat16 [64, 1024], P('roll', 'tensor'), may hold values from -5 to 5
- prefix_value: bfloat16 [64, 1024], P('roll', 'tensor'), may hold values from -5 to 5
- lengths: int32 [16], P('roll'), may hold values from 1 to 384
Outputs:
- grad_query: bfloat16 [6144, 4096], P('roll', 'tensor')
- grad_resp_key: bfloat16 [6144, 1024], P('roll', 'tensor')
- grad_resp_value: bfloat16 [6144, 1024], P('roll', 'tensor')
- grad_prefix_key: float32 [64, 1024], P('roll', 'tensor')
- grad_prefix_value: float32 [64, 1024], P('roll', 'tensor')
All inputs are finite; a program needn't handle non-finite values.
Results may differ from a plain program's by a relative error of at most 0.0063.
Values may be sent and summed in bfloat16 or wider, within the bound.
A program may use at most 128 MiB of HBM per device.

v0:
```python
from functools import partial

import jax
import jax.numpy as jnp
from jax import lax
from jax.sharding import PartitionSpec as P

HD = 128
ROWS = 384


def block_terms(query_rows, grad_rows, offset, all_keys, all_values, prefix_rows, keep_prefix):
    row_count = query_rows.shape[0]
    local_heads = all_keys.shape[1] // HD
    group_size = query_rows.shape[1] // all_keys.shape[1]
    score_scale = HD ** (-0.5)
    query_heads = query_rows.reshape(row_count, local_heads, group_size, HD)
    grad_heads = grad_rows.reshape(row_count, local_heads, group_size, HD)
    key_heads = all_keys.reshape(-1, local_heads, HD)
    value_heads = all_values.reshape(-1, local_heads, HD)
    scores = (
        jnp.einsum("ikgd,jkd->kgij", query_heads, key_heads, preferred_element_type=jnp.float32)
        * score_scale
    )
    query_place = offset + jnp.arange(row_count, dtype=jnp.int32)[:, None]
    key_place = jnp.arange(key_heads.shape[0], dtype=jnp.int32)[None, :]
    allowed = (key_place < prefix_rows) | (key_place - prefix_rows <= query_place)
    scores = jnp.where(allowed, scores, -jnp.inf)
    row_max = jnp.max(scores, axis=-1, keepdims=True)
    shifted = jnp.exp(scores - row_max)
    row_total = jnp.sum(shifted, axis=-1, keepdims=True)
    soft_weights = shifted / row_total
    weights_low = soft_weights.astype(jnp.bfloat16)
    prob_grad = jnp.einsum(
        "ikgd,jkd->kgij", grad_heads, value_heads, preferred_element_type=jnp.float32
    )
    row_delta = jnp.sum(soft_weights * prob_grad, axis=-1, keepdims=True)
    score_low = (soft_weights * (prob_grad - row_delta) * score_scale).astype(jnp.bfloat16)
    query_grad = jnp.einsum(
        "kgij,jkd->ikgd", score_low, key_heads, preferred_element_type=jnp.float32
    )
    query_grad = query_grad.reshape(row_count, -1).astype(jnp.bfloat16)
    score_low = score_low[:, :, :, prefix_rows:]
    weights_low = weights_low[:, :, :, prefix_rows:]
    key_count = score_low.shape[-1]
    key_grad = jnp.einsum(
        "kgij,ikgd->jkd", score_low, query_heads, preferred_element_type=jnp.float32
    )
    value_grad = jnp.einsum(
        "kgij,ikgd->jkd", weights_low, grad_heads, preferred_element_type=jnp.float32
    )
    return (
        query_grad,
        key_grad.reshape(key_count, -1),
        value_grad.reshape(key_count, -1),
        row_max,
        row_total,
        row_delta,
    )


def owner_block(query_rows, grad_rows, key_rows, value_rows, row_max, row_total, row_delta):
    row_count = query_rows.shape[0]
    local_heads = key_rows.shape[1] // HD
    group_size = query_rows.shape[1] // key_rows.shape[1]
    score_scale = HD ** (-0.5)
    query_heads = query_rows.reshape(row_count, local_heads, group_size, HD)
    grad_heads = grad_rows.reshape(row_count, local_heads, group_size, HD)
    key_heads = key_rows.reshape(-1, local_heads, HD)
    value_heads = value_rows.reshape(-1, local_heads, HD)
    scores = (
        jnp.einsum("ikgd,jkd->kgij", query_heads, key_heads, preferred_element_type=jnp.float32)
        * score_scale
    )
    soft_weights = jnp.exp(scores - row_max) / row_total
    weights_low = soft_weights.astype(jnp.bfloat16)
    prob_grad = jnp.einsum(
        "ikgd,jkd->kgij", grad_heads, value_heads, preferred_element_type=jnp.float32
    )
    score_low = (soft_weights * (prob_grad - row_delta) * score_scale).astype(jnp.bfloat16)
    key_count = key_rows.shape[0]
    key_grad = jnp.einsum(
        "kgij,ikgd->jkd", score_low, query_heads, preferred_element_type=jnp.float32
    )
    value_grad = jnp.einsum(
        "kgij,ikgd->jkd", weights_low, grad_heads, preferred_element_type=jnp.float32
    )
    return jnp.concatenate(
        [key_grad.reshape(key_count, -1), value_grad.reshape(key_count, -1)], axis=1
    )


def body(grad_out, out_weight, queries, resp_key, resp_value, prefix_key, prefix_value, lengths):
    rows_here = queries.shape[0]
    responses = rows_here // ROWS
    full_grad = lax.all_gather(grad_out, "tensor", axis=1, tiled=True)
    projected = jnp.dot(
        full_grad,
        lax.all_gather(out_weight, "roll", axis=0, tiled=True),
        preferred_element_type=jnp.float32,
    )
    position = jnp.arange(rows_here, dtype=jnp.int32)
    matches = (position // ROWS)[:, None] == jnp.arange(responses, dtype=jnp.int32)[None, :]
    row_limit = jnp.sum(jnp.where(matches, lengths[None, :], 0), axis=1)
    valid_rows = (position % ROWS < row_limit).astype(jnp.float32)
    out_grad = (projected * valid_rows[:, None]).astype(jnp.bfloat16)
    prefix_keys, prefix_values = (
        lax.all_gather(prefix_key, "roll", axis=0, tiled=True),
        lax.all_gather(prefix_value, "roll", axis=0, tiled=True),
    )
    prefix_rows = prefix_keys.shape[0]
    key_width = prefix_key.shape[1]
    block_rows = min(128, ROWS)
    query_parts, key_parts, value_parts, saved = ([], [], [], [])
    response = 0
    first_row = response * ROWS
    all_keys = jnp.concatenate([prefix_keys, resp_key], axis=0)
    all_values = jnp.concatenate([prefix_values, resp_value], axis=0)
    key_rows = ROWS
    key_sum = jnp.zeros((key_rows, key_width), jnp.float32)
    value_sum = jnp.zeros((key_rows, key_width), jnp.float32)
    for part_index in range(ROWS // block_rows):
        offset = part_index * block_rows
        start_row = first_row + offset
        compute_block = partial(
            block_terms,
            queries[start_row : start_row + block_rows],
            out_grad[start_row : start_row + block_rows],
            offset,
            all_keys,
            all_values,
            prefix_rows,
            False,
        )
        result = compute_block()
        query_grad, key_grad, value_grad, row_max, row_total, row_delta = result
        query_parts.append(query_grad)
        key_sum = key_sum + key_grad
        value_sum = value_sum + value_grad
        saved.append((response, offset, start_row, row_max, row_total, row_delta))
    key_parts.append(key_sum.astype(jnp.bfloat16))
    value_parts.append(value_sum.astype(jnp.bfloat16))
    key_rows = prefix_keys
    running = jnp.zeros((prefix_key.shape[0] * lax.axis_size("roll"), 2 * key_width), jnp.float32)
    for record in saved:
        response, offset, first_row, row_max, row_total, row_delta = record
        compute_term = partial(
            owner_block,
            queries[first_row : first_row + block_rows],
            out_grad[first_row : first_row + block_rows],
            key_rows,
            prefix_values,
            row_max,
            row_total,
            row_delta,
        )
        block_term = compute_term()
        running = running + block_term
    stacked = lax.psum_scatter(running, "roll", scatter_dimension=0, tiled=True)
    grad_prefix_key = stacked[:, :key_width]
    grad_prefix_value = stacked[:, key_width:]
    grad_query = jnp.concatenate(query_parts, axis=0)
    grad_resp_key = key_parts[0]
    grad_resp_value = value_parts[0]
    return (grad_query, grad_resp_key, grad_resp_value, grad_prefix_key, grad_prefix_value)


def solution(mesh):
    placed = (
        P("roll", "tensor"),
        P("roll", "tensor"),
        P("roll", "tensor"),
        P("roll", "tensor"),
        P("roll", "tensor"),
        P("roll", "tensor"),
        P("roll", "tensor"),
        P("roll"),
    )
    return jax.shard_map(
        body,
        mesh=mesh,
        in_specs=placed,
        out_specs=(
            P("roll", "tensor"),
            P("roll", "tensor"),
            P("roll", "tensor"),
            P("roll", "tensor"),
            P("roll", "tensor"),
        ),
        check_vma=False,
    )
```

profile of v0, /device:TPU:0, one launch (start us, length us, event | category | flops | bytes accessed | tf_op | source)
XLA Modules:
  0.0 343.5 jit_solution(4563650195555674438)
XLA Ops:
  7.2 0.7 all-gather.5.cloned.1.call-update
  8.0 0.7 all-gather.7.cloned.1.call-update
  8.7 23.5 %all-gather.1 = bf16[16,4,512]{2,1,0:T(4,128)(2,1)S(1)} all-gather(bf16[1,4,512]{2,1,0:T(4,128)(2,1)} %bitcast.299), channel_id=1, replica_groups=mesh['roll'=16,'tensor'=2] {'roll'}, dimensions={0}, use_global_device_ids=true | all-gather | bytes 69632 | tf_op jit(solution)/shard_map/all_gather | solution.py:109
  32.3 17.9 %all-gather = bf16[16,4,512]{2,1,0:T(4,128)(2,1)S(1)} all-gather(bf16[1,4,512]{2,1,0:T(4,128)(2,1)} %bitcast.300), channel_id=1, replica_groups=mesh['roll'=16,'tensor'=2] {'roll'}, dimensions={0}, use_global_device_ids=true | all-gather | bytes 69632 | tf_op jit(solution)/shard_map/all_gather | solution.py:108
  51.1 0.9 reshape.145
  52.0 1.5 fusion.145
  56.5 0.8 fusion.17
  57.2 1.2 fusion.67
  59.8 1.7 fusion.13
  62.1 1.1 fusion.75
  63.2 1.0 fusion.71
  64.2 1.9 all-gather.5.cloned.1.call-done
  66.1 110.4 %all-gather.7.cloned.1.call-done = bf16[5120,2048]{1,0:T(8,128)(2,1)} async-done(((bf16[320,2048]{1,0:T(8,128)(2,1)}), bf16[5120,2048]{1,0:T(8,128)(2,1)}) %all-gather.7.cloned.1.call-update) | async-done | bytes 20971536 | tf_op jit(solution)/shard_map/all_gather | solution.py:99
  176.5 13.7 %fusion.18 = bf16[384,2048]{1,0:T(8,128)(2,1)S(1)} fusion(bf16[384,5120]{1,0:T(8,128)(2,1)} %all-gather.5.cloned.1.call-done, bf16[5120,2048]{1,0:T(8,128)(2,1)} %all-gather.7.cloned.1.call-done, f32[384]{0:T(512)S(1)} %fusion.137), kind=kOutput, calls=%fused_computation.34 | convolution fusion | flops 8054636544 | bytes 26478080 | tf_op jit(solution)/shard_map/dot_general | solution.py:97
  190.2 1.1 fusion.146
  191.8 3.7 %fusion.8 = (f32[4,4,128]{2,1,0:T(4,128)S(1)}, f32[4,4,128,448]{2,3,1,0:T(8,128)S(1)}, f32[4,448,128,4]{2,1,3,0:T(8,128)S(1)}) fusion(f32[4,4,128]{2,1,0:T(4,128)S(1)} %get-tuple-element.51, f32[4,4,128]{2,1,0:T(4,128)S(1)} %get-tuple-element.48, f32[4,448,128,4]{2,1,3,0:T(8,128)} %copy-done.4, pred[128,448]{0,1:T(8,128)(4,1)S(1)} %get-tuple-element.39, ...), kind=kOutput, calls=%fused_computation.16 | convolution fusion | flops 240384000 | bytes 12075008 | tf_op jit(solution)/shard_map/ikgd,jkd->kgij/dot_general | solution.py:34
  196.1 1.2 copy-done.5
  197.2 1.3 convolution_convert_fusion.2
  198.6 1.5 fusion.34
  200.1 1.4 reshape.150
  201.5 1.4 reshape.148
  202.9 6.5 %fusion = (f32[4,4,128]{2,1,0:T(4,128)S(1)}, f32[4,4,128,448]{2,3,1,0:T(8,128)}, f32[4,448,128,4]{2,1,3,0:T(8,128)}) fusion(f32[4,4,128]{2,1,0:T(4,128)S(1)} %fusion.17, f32[4,4,128]{2,1,0:T(4,128)S(1)} %get-tuple-element.42, f32[4,448,128,4]{2,1,3,0:T(8,128)} %copy-done.3, pred[128,448]{0,1:T(8,128)(4,1)S(1)} %get-tuple-element.41, ...), kind=kOutput, calls=%fused_computation.2 | convolution fusion | flops 240384000 | bytes 12075008 | tf_op jit(solution)/shard_map/ikgd,jkd->kgij/dot_general | solution.py:34
  209.4 0.9 convolution_bitcast_fusion.3
  210.5 1.7 fusion.84
  212.2 2.2 fusion.82
  214.4 3.6 %fusion.31 = f32[4,128,384]{2,1,0:T(8,128)} fusion(f32[4,4,128,448]{2,3,1,0:T(8,128)} %get-tuple-element.30, bf16[128,4,4,128]{3,2,1,0:T(4,128)(2,1)S(1)} %reshape.150), kind=kOutput, calls=%fused_computation.48 | convolution fusion | flops 201326592 | bytes 2883584 | tf_op jit(solution)/shard_map/kgij,ikgd->jkd/dot_general | solution.py:49
  218.0 2.7 fusion.3
  220.7 1.3 copy-done
  222.5 1.0 copy.159
  223.5 0.7 copy.362
  224.2 6.3 %fusion.4 = (f32[4,4,128]{2,1,0:T(4,128)S(1)}, f32[4,4,128,448]{2,3,1,0:T(8,128)}, f32[4,448,128,4]{2,1,3,0:T(8,128)}) fusion(f32[4,4,128]{2,1,0:T(4,128)S(1)} %copy-done.24, f32[4,4,128]{2,1,0:T(4,128)S(1)} %get-tuple-element.45, f32[4,448,128,4]{2,1,3,0:T(8,128)} %copy-done.2, pred[128,448]{0,1:T(8,128)(4,1)S(1)} %get-tuple-element.40, ...), kind=kOutput, calls=%fused_computation.9 | convolution fusion | flops 240384000 | bytes 12075008 | tf_op jit(solution)/shard_map/ikgd,jkd->kgij/dot_general | solution.py:34
  230.7 0.7 copy.360
  231.4 1.1 fusion.83
  232.5 3.6 %fusion.32 = f32[4,128,384]{2,1,0:T(8,128)} fusion(f32[4,4,128,448]{2,3,1,0:T(8,128)} %get-tuple-element.28, bf16[128,4,4,128]{3,2,1,0:T(4,128)(2,1)S(1)} %reshape.148), kind=kOutput, calls=%fused_computation.49 | convolution fusion | flops 201326592 | bytes 2883584 | tf_op jit(solution)/shard_map/kgij,ikgd->jkd/dot_general | solution.py:49
  236.1 2.7 fusion.7
  238.8 0.7 copy.361
  239.5 1.3 convolution_convert_fusion.1
  240.8 2.1 copy.158
  242.8 1.0 copy_bitcast_fusion
  243.8 1.8 fusion.106
  245.6 1.9 fusion.46
  248.2 2.1 copy.157
  250.4 3.3 fusion.51
  253.7 1.2 pad_maximum_fusion
  255.0 1.9 copy.194
  256.9 0.9 copy.193
  257.8 77.7 %all-reduce.3.cloned.1.call-done = f32[64,1024]{1,0:T(8,128)} async-done(((f32[64,1024]{1,0:T(8,128)}), f32[64,1024]{1,0:T(8,128)}) %all-reduce.3.cloned.1.call-update) | async-done | bytes 262160
  335.5 1.4 fusion.147
  (81 shorter events, 7.3 us)
Async XLA Ops:
  7.2 43.7 %copy-start.21 = (bf16[384,512]{1,0:T(8,128)(2,1)S(1)}, bf16[384,512]{1,0:T(8,128)(2,1)}, u32[]{:S(2)}) copy-start(bf16[384,512]{1,0:T(8,128)(2,1)} %param.11) | copy-start | bytes 1179652
  7.2 43.9 %copy-start.22 = (bf16[384,512]{1,0:T(8,128)(2,1)S(1)}, bf16[384,512]{1,0:T(8,128)(2,1)}, u32[]{:S(2)}) copy-start(bf16[384,512]{1,0:T(8,128)(2,1)} %param.12) | copy-start | bytes 1179652
  7.2 58.9 %all-gather.5.cloned.1.call-start = ((), (), s32[]{:S(2)}) async-start(), calls=%async_computation | async-start | bytes 5898240 | tf_op jit(solution)/shard_map/all_gather | solution.py:96
  7.9 168.5 %all-gather.7.cloned.1.call-start = ((), (), s32[]{:S(2)}) async-start(), calls=%async_computation.1 | async-start | bytes 22282240 | tf_op jit(solution)/shard_map/all_gather | solution.py:99
  8.7 326.9 %all-reduce.3.cloned.1.call-start = ((), (), s32[]{:S(2)}) async-start(), calls=%async_computation.2 | async-start | bytes 524288
  51.1 3.2 copy-start.25
  53.7 144.8 %copy-start.10 = (bf16[128,2048]{0,1:T(8,128)(2,1)}, bf16[128,2048]{0,1:T(8,128)(2,1)S(1)}, u32[]{:S(2)}) copy-start(bf16[128,2048]{0,1:T(8,128)(2,1)S(1)} %copy.267) | copy-start | bytes 1572868
  56.5 2.6 copy-start.3
  59.1 2.3 copy-start.2
  59.8 2.3 copy-start.4
  62.1 128.1 %copy-start.23 = (f32[4,4,128]{2,1,0:T(4,128)}, f32[4,4,128]{2,1,0:T(4,128)S(1)}, u32[]{:S(2)}) copy-start(f32[4,4,128]{2,1,0:T(4,128)S(1)} %get-tuple-element.52) | copy-start | bytes 24580
  191.7 18.8 %copy-start.8 = (bf16[128,4,4,128]{3,2,1,0:T(4,128)(2,1)}, bf16[128,4,4,128]{3,2,1,0:T(4,128)(2,1)S(1)}, u32[]{:S(2)}) copy-start(bf16[128,4,4,128]{3,2,1,0:T(4,128)(2,1)S(1)} %reshape.146) | copy-start | bytes 1572868
  195.5 1.8 copy-start.5
  202.9 6.5 %copy-start.14 = (f32[4,4,128,64]{2,3,1,0:T(8,128)S(1)}, f32[4,4,128,64]{2,3,1,0:T(8,128)}, u32[]{:S(2)}) copy-start(f32[4,4,128,64]{2,3,1,0:T(8,128)} %fusion.67) | copy-start | bytes 1572868
  202.9 7.4 %copy-start.15 = (f32[4,4,128,64]{2,3,1,0:T(8,128)S(1)}, f32[4,4,128,64]{2,3,1,0:T(8,128)}, u32[]{:S(2)}) copy-start(f32[4,4,128,64]{2,3,1,0:T(8,128)} %fusion.75) | copy-start | bytes 1572868
  214.4 3.6 %copy-start.6 = (f32[4,4,128,448]{2,3,1,0:T(8,128)S(1)}, f32[4,4,128,448]{2,3,1,0:T(8,128)}, u32[]{:S(2)}) copy-start(f32[4,4,128,448]{2,3,1,0:T(8,128)} %get-tuple-element.30) | copy-start | bytes 11010052
  220.7 1.3 copy-start
  222.0 2.2 copy-start.20
  222.0 2.2 copy-start.24
  224.2 6.3 %copy-start.13 = (f32[4,4,128,64]{2,3,1,0:T(8,128)S(1)}, f32[4,4,128,64]{2,3,1,0:T(8,128)}, u32[]{:S(2)}) copy-start(f32[4,4,128,64]{2,3,1,0:T(8,128)} %fusion.71) | copy-start | bytes 1572868
  232.5 3.6 %copy-start.7 = (f32[4,4,128,448]{2,3,1,0:T(8,128)S(1)}, f32[4,4,128,448]{2,3,1,0:T(8,128)}, u32[]{:S(2)}) copy-start(f32[4,4,128,448]{2,3,1,0:T(8,128)} %get-tuple-element.28) | copy-start | bytes 11010052
  236.1 2.7 copy-start.19
  245.6 1.9 copy-start.1
  247.5 2.8 copy-start.9
  247.5 2.8 copy-start.11
  247.5 2.8 copy-start.12
  248.2 5.5 %copy-start.16 = (bf16[128,2048]{1,0:T(8,128)(2,1)S(1)}, bf16[128,2048]{1,0:T(8,128)(2,1)}, u32[]{:S(2)}) copy-start(bf16[128,2048]{1,0:T(8,128)(2,1)} %copy.159) | copy-start | bytes 1572868
  248.2 5.5 %copy-start.17 = (bf16[128,2048]{1,0:T(8,128)(2,1)S(1)}, bf16[128,2048]{1,0:T(8,128)(2,1)}, u32[]{:S(2)}) copy-start(bf16[128,2048]{1,0:T(8,128)(2,1)} %copy.158) | copy-start | bytes 1572868
  250.3 3.4 copy-start.18
Sparse Core Ops, SparseCore 0:
  9.5 56.4 all-gather.4
  67.7 108.7 all-gather.6
  245.8 89.7 all-reduce.2
where the time goes:
time: 344 us; the launch traced here: 343 us
  waiting for transfers between devices  191 us (56%)
  matrix products  59.4 us (17%)
  blocking collectives  41.4 us (12%)
  local copies, waits for them, and re-layouts  23.9 us (7%)
  between operations  15.5 us (5%)
  other arithmetic  11.8 us (3%)
    all_gather x1, waiting for transfers between devices, body(): lax.all_gather(out_weight, 'roll', axis=0, tiled=True)  110 us
    unnamed x4, waiting for transfers between devices  79.1 us
    all_gather x1, blocking collectives, body(): lax.all_gather(prefix_value, 'roll', axis=0, tiled=True)  23.5 us
    all_gather x1, blocking collectives, body(): lax.all_gather(prefix_key, 'roll', axis=0, tiled=True)  17.9 us
    dot_general x3, matrix products, block_terms(): jnp.einsum('ikgd,jkd->kgij', grad_heads, value_heads, preferred_element_t...  16.5 us
    dot_general x1, matrix products, body(): jnp.dot(full_grad, lax.all_gather(out_weight, 'roll', axis=0, tiled=True)...  13.7 us
    dot_general x3, matrix products, block_terms(): jnp.einsum('kgij,ikgd->jkd', weights_low, grad_heads, preferred_element_t...  10.5 us
    unnamed x60, local copies, waits for them, and re-layouts  7.47 us
  transfers between devices with their start and end apart: 3, of which 3 were waited for; matrix products, arithmetic and copies ran while one was open for 7% of the time, Pallas kernels for 0%

commit v1 on v0

v1 whole, which is shorter than its diff:
```python
import functools

import jax
import jax.numpy as jnp
from jax import lax
from jax.experimental import pallas as pl
from jax.experimental.pallas import tpu as pltpu
from jax.sharding import PartitionSpec as P

HD = 128
MESH = pl.DeviceIdType.MESH
NT = (((1,), (1,)), ((), ()))
TN = (((0,), (0,)), ((), ()))


def grid_of(roll):
    cores = 2 if roll % 2 == 0 else 1
    chips = roll // cores
    ys = 1
    while 4 * ys * ys <= chips and chips % (2 * ys) == 0:
        ys *= 2
    return chips // ys, ys, cores


def kernel(
    R, T,
    len_ref, g_hbm, w_hbm, pkv_hbm, q_ref, k_ref, v_ref,
    oq_ref, ok_ref, ov_ref, opk_ref, opv_ref,
    wbuf, gbuf, pbuf, pfull, og, dk, dv, rs_src, rs_in,
    lsem, glsem, plsem, rsem, ssem, grsem, gssem, prsem, pssem, rrsem, rssem,
):
    Z, Y, C = grid_of(R)
    NR, _, WR, SUB = wbuf.shape
    NK = rs_in.shape[0]
    PR = pbuf.shape[1]
    PF = R * PR
    rows = q_ref.shape[0]
    group = q_ref.shape[1] // k_ref.shape[1]
    gw = group * HD
    per_head = gw // SUB
    kw = k_ref.shape[1]
    me = lax.axis_index("roll")
    tp = lax.axis_index("tensor")
    c = lax.rem(me, C)
    y = lax.rem(me // C, Y)
    z = me // (C * Y)
    items = Z * Y
    lag = (Z - 1) + (Y - 1)
    every = 6

    def rid(zz, yy, cc):
        return (zz * Y + yy) * C + cc

    own_w = [
        pltpu.make_async_copy(w_hbm.at[:, pl.ds(r * SUB, SUB)], wbuf.at[r, me], lsem.at[r])
        for r in range(NR)
    ]
    own_g = pltpu.make_async_copy(g_hbm, gbuf.at[tp], glsem)
    own_p = pltpu.make_async_copy(pkv_hbm, pbuf.at[me], plsem)
    for cp in own_w:
        cp.start()
    own_g.start()
    own_p.start()

    barrier = pltpu.get_barrier_semaphore()

    @pl.loop(1, R)
    def _(d):
        pl.semaphore_signal(
            barrier, inc=1, device_id={"roll": lax.rem(me + d, R)}, device_id_type=MESH)

    for t in range(1, T):
        pl.semaphore_signal(
            barrier, inc=1, device_id={"tensor": lax.rem(tp + t, T)}, device_id_type=MESH)
    pl.semaphore_wait(barrier, R - 1 + T - 1)

    def w_copy(kind, j, r, o, dst):
        return pltpu.make_async_remote_copy(
            src_ref=wbuf.at[r, o], dst_ref=wbuf.at[r, o],
            send_sem=ssem.at[kind, r, j], recv_sem=rsem.at[r, o],
            device_id={"roll": dst}, device_id_type=MESH)

    def place(j):
        return lax.rem(z + j // Y, Z), lax.rem(y + lax.rem(j, Y), Y)

    def sends(j, r, act):
        zz, yy = place(j)
        o = rid(zz, yy, c)
        crossed = lax.rem(r, every) == every // 2
        along_z = jnp.logical_or(yy == y, crossed)
        along_y = jnp.logical_or(zz == z, jnp.logical_not(crossed))

        def step(kind, cond, dst):
            @pl.when(cond)
            def _():
                act(w_copy(kind, j, r, o, dst))

        if Y > 1:
            step(0, along_y & (yy <= y) & (y + 1 < Y), rid(z, y + 1, c))
            step(1, along_y & (yy >= y) & (y > 0), rid(z, y - 1, c))
        if Z > 1:
            step(2, along_z & (zz <= z) & (z + 1 < Z), rid(z + 1, y, c))
            step(3, along_z & (zz >= z) & (z > 0), rid(z - 1, y, c))
        if C > 1:
            act(w_copy(4, j, r, o, rid(z, y, 1 - c)))

    def g_copy(t):
        return pltpu.make_async_remote_copy(
            src_ref=gbuf.at[tp], dst_ref=gbuf.at[tp], send_sem=gssem.at[t],
            recv_sem=grsem.at[tp], device_id={"tensor": lax.rem(tp + t, T)},
            device_id_type=MESH)

    def g_arrival(t):
        src = lax.rem(tp + t, T)
        return pltpu.make_async_remote_copy(
            src_ref=gbuf.at[src], dst_ref=gbuf.at[src], send_sem=gssem.at[t],
            recv_sem=grsem.at[src], device_id={"tensor": src}, device_id_type=MESH)

    def p_copy(slot, d, o):
        return pltpu.make_async_remote_copy(
            src_ref=pbuf.at[slot], dst_ref=pbuf.at[slot], send_sem=pssem.at[d],
            recv_sem=prsem.at[slot], device_id={"roll": o}, device_id_type=MESH)

    def r_copy(h, src, slot, o):
        return pltpu.make_async_remote_copy(
            src_ref=rs_src.at[h, src], dst_ref=rs_in.at[h, slot], send_sem=rssem.at[h, src],
            recv_sem=rrsem.at[h, slot], device_id={"roll": o}, device_id_type=MESH)

    def project(r):
        total = None
        for t in range(T):
            n = R // T
            part = jnp.dot(
                gbuf[t], wbuf[r, t * n:(t + 1) * n].reshape(n * WR, SUB),
                preferred_element_type=jnp.float32)
            total = part if total is None else total + part
        row = lax.broadcasted_iota(jnp.int32, (rows, SUB), 0)
        valid = (row < len_ref[0]).astype(jnp.float32)
        og[lax.rem(r, per_head)] = (total * valid).astype(jnp.bfloat16)

    def attend(h):
        scale = HD ** -0.5
        power = scale * 1.4426950408889634
        kcols = pl.ds(pl.multiple_of(h * HD, HD), HD)
        vcols = pl.ds(pl.multiple_of(kw + h * HD, HD), HD)
        kall = jnp.concatenate([pfull[:, kcols].astype(jnp.bfloat16), k_ref[:, kcols]], axis=0)
        vall = jnp.concatenate([pfull[:, vcols].astype(jnp.bfloat16), v_ref[:, kcols]], axis=0)
        br = min(128, rows)
        nb = rows // br
        key = lax.broadcasted_iota(jnp.int32, (br, group * br), 0)
        row = lax.rem(lax.broadcasted_iota(jnp.int32, (br, group * br), 1), br)
        allowed = key <= row
        for i in range(nb - 1, -1, -1):
            span = slice(i * br, (i + 1) * br)
            nk = PF + (i + 1) * br
            kc, vc = kall[:nk], vall[:nk]
            qs, gs = [], []
            for a in range(group):
                qs.append(q_ref[span, pl.ds(pl.multiple_of(h * gw + a * HD, HD), HD)])
                lane = a * HD
                gs.append(og[lane // SUB, span, lane % SUB:lane % SUB + HD])
            qi = jnp.concatenate(qs, axis=0)
            gi = jnp.concatenate(gs, axis=0)
            s = lax.dot_general(kc, qi, NT, preferred_element_type=jnp.float32)
            s = jnp.concatenate([s[:nk - br], jnp.where(allowed, s[nk - br:], -jnp.inf)], axis=0)
            top = jnp.max(s, axis=0, keepdims=True)
            e = jnp.exp2((s - top) * power)
            inv = 1.0 / jnp.sum(e, axis=0, keepdims=True)
            dp = lax.dot_general(vc, gi, NT, preferred_element_type=jnp.float32)
            w = e * inv
            delta = jnp.sum(w * dp, axis=0, keepdims=True)
            wl = w.astype(jnp.bfloat16)
            ds = (w * (dp - delta) * scale).astype(jnp.bfloat16)
            dki = jnp.dot(ds, qi, preferred_element_type=jnp.float32)
            dvi = jnp.dot(wl, gi, preferred_element_type=jnp.float32)
            if i == nb - 1:
                dk[...] = dki
                dv[...] = dvi
            else:
                dk[:nk] += dki
                dv[:nk] += dvi
            dq = lax.dot_general(kc, ds, TN, preferred_element_type=jnp.float32).T
            for a in range(group):
                oq_ref[span, pl.ds(pl.multiple_of(h * gw + a * HD, HD), HD)] = (
                    dq[a * br:(a + 1) * br].astype(jnp.bfloat16))
        for o in range(R):
            rs_src[h, o, :, :HD] = dk[o * PR:(o + 1) * PR]
            rs_src[h, o, :, HD:] = dv[o * PR:(o + 1) * PR]
        ok_ref[:, kcols] = dk[PF:].astype(jnp.bfloat16)
        ov_ref[:, kcols] = dv[PF:].astype(jnp.bfloat16)
        rs_in[h, me] = rs_src[h, me]

        @pl.loop(1, R)
        def _(d):
            o = lax.rem(me + d, R)
            r_copy(h, o, me, o).start()

    own_p.wait()
    own_g.wait()
    for cp in own_w:
        cp.wait()

    def step(s, carry):
        def one(j, carry):
            zz, yy = place(j)
            r = s - jnp.abs(zz - z) - jnp.abs(yy - y)

            @pl.when((r >= 0) & (r < NR))
            def _():
                @pl.when(j > 0)
                def _():
                    w_copy(4, j, r, rid(zz, yy, c), rid(z, y, 1 - c)).wait_recv()

                sends(j, r, lambda cp: cp.start())

            return carry

        lax.fori_loop(0, items, one, 0)

        @pl.when(s == 0)
        def _():
            for t in range(1, T):
                g_copy(t).start()

            @pl.loop(1, R)
            def _(d):
                p_copy(me, d, lax.rem(me + d, R)).start()

        ready = s - lag

        @pl.when(ready >= 0)
        def _():
            if C > 1:
                @pl.loop(0, items)
                def _(j):
                    zz, yy = place(j)
                    w_copy(4, j, ready, rid(zz, yy, 1 - c), rid(z, y, 1 - c)).wait_recv()

            @pl.when(ready == 0)
            def _():
                for t in range(1, T):
                    g_arrival(t).wait_recv()

                @pl.loop(1, R)
                def _(d):
                    o = lax.rem(me + d, R)
                    p_copy(o, d, o).wait_recv()

                for o in range(R):
                    pfull[o * PR:(o + 1) * PR, :] = pbuf[o].astype(jnp.float32)

            project(ready)

            @pl.when(lax.rem(ready, per_head) == per_head - 1)
            def _():
                attend(ready // per_head)

        return carry

    lax.fori_loop(0, NR + lag, step, 0)

    @pl.loop(0, NK)
    def _(h):
        @pl.loop(1, R)
        def _(d):
            o = lax.rem(me + d, R)
            r_copy(h, o, o, o).wait_recv()

    for h in range(NK):
        total = rs_in[h, 0]
        for o in range(1, R):
            total = total + rs_in[h, o]
        opk_ref[:, h * HD:(h + 1) * HD] = total[:, :HD]
        opv_ref[:, h * HD:(h + 1) * HD] = total[:, HD:]

    @pl.loop(0, NR)
    def _(r):
        @pl.loop(0, items)
        def _(j):
            sends(j, r, lambda cp: cp.wait_send())

    for t in range(1, T):
        g_copy(t).wait_send()

    @pl.loop(1, R)
    def _(d):
        o = lax.rem(me + d, R)
        p_copy(me, d, o).wait_send()

        @pl.loop(0, NK)
        def _(h):
            r_copy(h, o, me, o).wait_send()


def body(R, T, grad_out, out_weight, queries, resp_key, resp_value, prefix_key, prefix_value, lengths):
    rows, dcols = grad_out.shape
    wr, cols = out_weight.shape
    kw = resp_key.shape[1]
    pr = prefix_key.shape[0]
    nk = kw // HD
    gw = cols // nk
    sub = gw // 2 if gw % 256 == 0 else gw
    nr = cols // sub
    Z, Y, C = grid_of(R)
    vm = pl.BlockSpec(memory_space=pltpu.VMEM)
    hb = pl.BlockSpec(memory_space=pl.ANY)
    dma = pltpu.SemaphoreType.DMA
    pkv = jnp.concatenate([prefix_key, prefix_value], axis=1)
    bf, f32 = jnp.bfloat16, jnp.float32
    return pl.pallas_call(
        functools.partial(kernel, R, T),
        out_shape=(
            jax.ShapeDtypeStruct((rows, cols), bf),
            jax.ShapeDtypeStruct((rows, kw), bf),
            jax.ShapeDtypeStruct((rows, kw), bf),
            jax.ShapeDtypeStruct((pr, kw), f32),
            jax.ShapeDtypeStruct((pr, kw), f32),
        ),
        in_specs=[pl.BlockSpec(memory_space=pltpu.SMEM), hb, hb, hb, vm, vm, vm],
        out_specs=(vm,) * 5,
        scratch_shapes=[
            pltpu.VMEM((nr, R, wr, sub), bf),
            pltpu.VMEM((T, rows, dcols), bf),
            pltpu.VMEM((R, pr, 2 * kw), bf),
            pltpu.VMEM((R * pr, 2 * kw), f32),
            pltpu.VMEM((gw // sub, rows, sub), bf),
            pltpu.VMEM((R * pr + rows, HD), f32),
            pltpu.VMEM((R * pr + rows, HD), f32),
            pltpu.VMEM((nk, R, pr, 2 * HD), f32),
            pltpu.VMEM((nk, R, pr, 2 * HD), f32),
            dma((nr,)), dma, dma,
            dma((nr, R)), dma((5, nr, Z * Y)),
            dma((T,)), dma((T,)),
            dma((R,)), dma((R,)),
            dma((nk, R)), dma((nk, R)),
        ],
        compiler_params=pltpu.CompilerParams(
            collective_id=0, has_side_effects=True, vmem_limit_bytes=60 * 1024 * 1024),
        name="gather_project_attend",
    )(lengths, grad_out, out_weight, pkv, queries, resp_key, resp_value)


def solution(mesh):
    spec = P("roll", "tensor")
    return jax.shard_map(
        functools.partial(body, mesh.shape["roll"], mesh.shape["tensor"]),
        mesh=mesh,
        in_specs=(spec,) * 7 + (P("roll"),),
        out_specs=(spec,) * 5,
        check_vma=False,
    )
```

time: 344 us -> 143 us (0.42)
  waiting for transfers between devices: 191 us -> 0 us
  Pallas kernels: 0 us -> 134 us
  matrix products: 59.4 us -> 0 us
  blocking collectives: 41.4 us -> 0 us
  local copies, waits for them, and re-layouts: 23.9 us -> 5.5 us
  between operations: 15.5 us -> 1.31 us
  other arithmetic: 11.8 us -> 1.31 us
    pallas_call x0 -> x1, Pallas kernels: none -> 134 us  [body(): pl.pallas_call(functools.partial(kernel, R, T), out_shape=(jax.ShapeDtype...]
    all_gather x2 -> x0, waiting for transfers between devices: 112 us -> none  [the longest x1 110 us: body(): lax.all_gather(out_weight, 'roll', axis=0, tiled=True)]
    unnamed x4 -> x0, waiting for transfers between devices: 79.1 us -> none
    dot_general x25 -> x0, matrix products: 59.4 us -> none  [the longest x3 16.5 us: block_terms(): jnp.einsum('ikgd,jkd->kgij', grad_heads, value_heads, preferred_element_t...]
    all_gather x2 -> x0, blocking collectives: 41.4 us -> none  [the longest x1 23.5 us: body(): lax.all_gather(prefix_value, 'roll', axis=0, tiled=True)]
    reshape x12 -> x0, local copies, waits for them, and re-layouts: 7.21 us -> none  [the longest x3 3.17 us: block_terms(): grad_heads = grad_rows.reshape(row_count, local_heads, group_size, HD)]
    convert_element_type x4 -> x0, other arithmetic: 6.03 us -> none  [the longest x3 6.02 us: block_terms(): (soft_weights * (prob_grad - row_delta) * score_scale).astype(jnp.bfloat16)]
    convert_element_type x3 -> x0, local copies, waits for them, and re-layouts: 5.2 us -> none  [block_terms(): query_grad = query_grad.reshape(row_count, -1).astype(jnp.bfloat16)]
  transfers between devices with their start and end apart: 3 -> 0, of which waited for: 3 -> 0; matrix products, arithmetic and copies ran while one was open for 7% -> 0% of each run, Pallas kernels for 0% -> 0%
where the time goes in v1:
time: 143 us; the launch traced here: 142 us
  Pallas kernels  134 us (94%)
  local copies, waits for them, and re-layouts  5.5 us (4%)
    pallas_call x1, Pallas kernels, body(): pl.pallas_call(functools.partial(kernel, R, T), out_shape=(jax.ShapeDtype...  134 us
    unnamed x13, local copies, waits for them, and re-layouts  5.5 us

profile of v1, /device:TPU:0, one launch (start us, length us, event | category | flops | bytes accessed | tf_op | source)
XLA Modules:
  0.0 142.3 jit_solution(12055134312405673729)
XLA Ops:
  1.3 1.3 pad_maximum_fusion.pkv_hbm
  2.6 134.2 %gather_project_attend.1 = (bf16[384,2048]{1,0:T(8,128)(2,1)}, bf16[384,512]{1,0:T(8,128)(2,1)}, bf16[384,512]{1,0:T(8,128)(2,1)}, f32[4,512]{1,0:T(4,128)}, f32[4,512]{1,0:T(4,128)}) custom-call(s32[1]{0:T(128)S(6)} %copy.18.len_ref, bf16[384,2560]{1,0:T(8,128)(2,1)} %g_hbm.1, bf16[320,2048]{1,0:T(8,128)(2,1)} %w_hbm.1, ...), custom_call_target="tpu_custom_call" | custom-call | tf_op jit(solution)/shard_map/gather_project_attend/pallas_call | solution.py:310
  136.8 0.0 copy-start.1
  136.8 0.0 copy-start
  136.8 2.8 %copy.19 = bf16[384,2048]{1,0:T(8,128)(2,1)} copy(bf16[384,2048]{1,0:T(8,128)(2,1)} %get-tuple-element.10) | data formatting | bytes 3145728
  139.6 0.0 copy-done.1
  139.6 0.0 copy-start.3
  139.6 0.0 copy-start.2
  139.6 0.7 copy.20
  140.4 0.0 copy-done
  140.4 0.7 copy.21
  141.1 0.0 copy-done.3
  141.1 0.6 copy.22
  141.7 0.0 copy-done.2
  141.7 0.6 copy.23
Async XLA Ops:
  136.8 2.8 %copy-start.1 = (bf16[384,512]{1,0:T(8,128)(2,1)S(1)}, bf16[384,512]{1,0:T(8,128)(2,1)}, u32[]{:S(2)}) copy-start(bf16[384,512]{1,0:T(8,128)(2,1)} %get-tuple-element.11) | copy-start | bytes 1179652
  136.8 3.6 %copy-start = (bf16[384,512]{1,0:T(8,128)(2,1)S(1)}, bf16[384,512]{1,0:T(8,128)(2,1)}, u32[]{:S(2)}) copy-start(bf16[384,512]{1,0:T(8,128)(2,1)} %get-tuple-element.12) | copy-start | bytes 1179652
  139.6 1.5 %copy-start.3 = (f32[4,512]{1,0:T(4,128)S(1)}, f32[4,512]{1,0:T(4,128)}, u32[]{:S(2)}) copy-start(f32[4,512]{1,0:T(4,128)} %get-tuple-element.13) | copy-start | bytes 24580
  139.6 2.1 %copy-start.2 = (f32[4,512]{1,0:T(4,128)S(1)}, f32[4,512]{1,0:T(4,128)}, u32[]{:S(2)}) copy-start(f32[4,512]{1,0:T(4,128)} %get-tuple-element.14) | copy-start | bytes 24580

commit v2 on v1

--- a/solution.py
+++ b/solution.py
@@ -24,7 +24,7 @@
 
 def kernel(
     R, T,
-    len_ref, g_hbm, w_hbm, pkv_hbm, q_ref, k_ref, v_ref,
+    len_ref, g_hbm, w_hbm, pk_hbm, pv_hbm, q_ref, k_ref, v_ref,
     oq_ref, ok_ref, ov_ref, opk_ref, opv_ref,
     wbuf, gbuf, pbuf, pfull, og, dk, dv, rs_src, rs_in,
     lsem, glsem, plsem, rsem, ssem, grsem, gssem, prsem, pssem, rrsem, rssem,
@@ -56,11 +56,15 @@
         for r in range(NR)
     ]
     own_g = pltpu.make_async_copy(g_hbm, gbuf.at[tp], glsem)
-    own_p = pltpu.make_async_copy(pkv_hbm, pbuf.at[me], plsem)
+    own_p = [
+        pltpu.make_async_copy(pk_hbm, pbuf.at[me, :, pl.ds(0, kw)], plsem.at[0]),
+        pltpu.make_async_copy(pv_hbm, pbuf.at[me, :, pl.ds(kw, kw)], plsem.at[1]),
+    ]
     for cp in own_w:
         cp.start()
     own_g.start()
-    own_p.start()
+    for cp in own_p:
+        cp.start()
 
     barrier = pltpu.get_barrier_semaphore()
 
@@ -195,7 +199,8 @@
             o = lax.rem(me + d, R)
             r_copy(h, o, me, o).start()
 
-    own_p.wait()
+    for cp in own_p:
+        cp.wait()
     own_g.wait()
     for cp in own_w:
         cp.wait()
@@ -290,6 +295,12 @@
         @pl.loop(0, NK)
         def _(h):
             r_copy(h, o, me, o).wait_send()
+
+
+def hand_out(*refs):
+    half = len(refs) // 2
+    for src, dst in zip(refs[:half], refs[half:]):
+        dst[...] = src[...]
 
 
 def body(R, T, grad_out, out_weight, queries, resp_key, resp_value, prefix_key, prefix_value, lengths):
@@ -305,9 +316,8 @@
     vm = pl.BlockSpec(memory_space=pltpu.VMEM)
     hb = pl.BlockSpec(memory_space=pl.ANY)
     dma = pltpu.SemaphoreType.DMA
-    pkv = jnp.concatenate([prefix_key, prefix_value], axis=1)
     bf, f32 = jnp.bfloat16, jnp.float32
-    return pl.pallas_call(
+    grads = pl.pallas_call(
         functools.partial(kernel, R, T),
         out_shape=(
             jax.ShapeDtypeStruct((rows, cols), bf),
@@ -316,7 +326,7 @@
             jax.ShapeDtypeStruct((pr, kw), f32),
             jax.ShapeDtypeStruct((pr, kw), f32),
         ),
-        in_specs=[pl.BlockSpec(memory_space=pltpu.SMEM), hb, hb, hb, vm, vm, vm],
+        in_specs=[pl.BlockSpec(memory_space=pltpu.SMEM), hb, hb, hb, hb, vm, vm, vm],
         out_specs=(vm,) * 5,
         scratch_shapes=[
             pltpu.VMEM((nr, R, wr, sub), bf),
@@ -328,7 +338,7 @@
             pltpu.VMEM((R * pr + rows, HD), f32),
             pltpu.VMEM((nk, R, pr, 2 * HD), f32),
             pltpu.VMEM((nk, R, pr, 2 * HD), f32),
-            dma((nr,)), dma, dma,
+            dma((nr,)), dma, dma((2,)),
             dma((nr, R)), dma((5, nr, Z * Y)),
             dma((T,)), dma((T,)),
             dma((R,)), dma((R,)),
@@ -337,7 +347,21 @@
         compiler_params=pltpu.CompilerParams(
             collective_id=0, has_side_effects=True, vmem_limit_bytes=60 * 1024 * 1024),
         name="gather_project_attend",
-    )(lengths, grad_out, out_weight, pkv, queries, resp_key, resp_value)
+    )(lengths, grad_out, out_weight, prefix_key, prefix_value, queries, resp_key, resp_value)
+    steps = 3 if rows % 48 == 0 else 1
+    specs = [
+        pl.BlockSpec((rows // steps, g.shape[1]), lambda i: (i, 0)) if g.shape[0] == rows
+        else pl.BlockSpec(g.shape, lambda i: (0, 0))
+        for g in grads
+    ]
+    return pl.pallas_call(
+        hand_out,
+        out_shape=tuple(jax.ShapeDtypeStruct(g.shape, g.dtype) for g in grads),
+        grid=(steps,),
+        in_specs=specs,
+        out_specs=tuple(specs),
+        name="hand_out",
+    )(*grads)
 
 
 def solution(mesh):

time: 143 us -> 140 us (0.979)
  local copies, waits for them, and re-layouts: 5.5 us -> 0 us
  Pallas kernels: 134 us -> 138 us
    unnamed x13 -> x0, local copies, waits for them, and re-layouts: 5.5 us -> none
    pallas_call x0 -> x1, Pallas kernels: none -> 3.87 us  [body(): pl.pallas_call(hand_out, out_shape=tuple((jax.ShapeDtypeStruct(g.shape, g...]
where the time goes in v2:
time: 140 us; the launch traced here: 139 us
  Pallas kernels  138 us (99%)
    pallas_call x1, Pallas kernels, body(): pl.pallas_call(functools.partial(kernel, R, T), out_shape=(jax.ShapeDtype...  134 us
    pallas_call x1, Pallas kernels, body(): pl.pallas_call(hand_out, out_shape=tuple((jax.ShapeDtypeStruct(g.shape, g...  3.87 us

profile of v2, /device:TPU:0, one launch (start us, length us, event | category | flops | bytes accessed | tf_op | source)
XLA Modules:
  0.0 139.4 jit_solution(9130650730827194241)
XLA Ops:
  1.3 134.3 %gather_project_attend.1 = (bf16[384,2048]{1,0:T(8,128)(2,1)}, bf16[384,512]{1,0:T(8,128)(2,1)}, bf16[384,512]{1,0:T(8,128)(2,1)}, f32[4,512]{1,0:T(4,128)}, f32[4,512]{1,0:T(4,128)}) custom-call(s32[1]{0:T(128)S(6)} %copy.13.len_ref, bf16[384,2560]{1,0:T(8,128)(2,1)} %g_hbm.1, bf16[320,2048]{1,0:T(8,128)(2,1)} %w_hbm.1, bf16[4,512]{1,0:T(4,128)(2,1)} %pk_hbm.1, ...), custom_call_target="tpu_custom_call" | custom-call | tf_op jit(solution)/shard_map/gather_project_attend/pallas_call | solution.py:320
  135.6 3.9 %hand_out.1 = (bf16[384,2048]{1,0:T(8,128)(2,1)}, bf16[384,512]{1,0:T(8,128)(2,1)}, bf16[384,512]{1,0:T(8,128)(2,1)}, f32[4,512]{1,0:T(4,128)}, f32[4,512]{1,0:T(4,128)}) custom-call(bf16[384,2048]{1,0:T(8,128)(2,1)} %get-tuple-element.10.refs_0_, bf16[384,512]{1,0:T(8,128)(2,1)} %get-tuple-element.11.refs_1_, bf16[384,512]{1,0:T(8,128)(2,1)} %get-tuple-element.12.refs_2_, ...), custom_call_target="tpu_custom_call" | custom-call | tf_op jit(solution)/shard_map/hand_out/pallas_call | solution.py:357

commit v3 on v2

--- a/solution.py
+++ b/solution.py
@@ -24,9 +24,9 @@
 
 def kernel(
     R, T,
-    len_ref, g_hbm, w_hbm, pk_hbm, pv_hbm, q_ref, k_ref, v_ref,
+    len_ref, g_hbm, w_hbm, pk_hbm, pv_hbm, q_hbm, k_hbm, v_hbm,
     oq_ref, ok_ref, ov_ref, opk_ref, opv_ref,
-    wbuf, gbuf, pbuf, pfull, og, dk, dv, rs_src, rs_in,
+    q_ref, k_ref, v_ref, qkvsem, wbuf, gbuf, pbuf, pfull, og, dk, dv, rs_src, rs_in,
     lsem, glsem, plsem, rsem, ssem, grsem, gssem, prsem, pssem, rrsem, rssem,
 ):
     Z, Y, C = grid_of(R)
@@ -63,6 +63,12 @@
     for cp in own_w:
         cp.start()
     own_g.start()
+    own_qkv = [
+        pltpu.make_async_copy(src, dst, qkvsem.at[i])
+        for i, (src, dst) in enumerate(((q_hbm, q_ref), (k_hbm, k_ref), (v_hbm, v_ref)))
+    ]
+    for cp in own_qkv:
+        cp.start()
     for cp in own_p:
         cp.start()
 
@@ -202,6 +208,8 @@
     for cp in own_p:
         cp.wait()
     own_g.wait()
+    for cp in own_qkv:
+        cp.wait()
     for cp in own_w:
         cp.wait()
 
@@ -326,9 +334,10 @@
             jax.ShapeDtypeStruct((pr, kw), f32),
             jax.ShapeDtypeStruct((pr, kw), f32),
         ),
-        in_specs=[pl.BlockSpec(memory_space=pltpu.SMEM), hb, hb, hb, hb, vm, vm, vm],
+        in_specs=[pl.BlockSpec(memory_space=pltpu.SMEM), hb, hb, hb, hb, hb, hb, hb],
         out_specs=(vm,) * 5,
         scratch_shapes=[
+            pltpu.VMEM((rows, cols), bf), pltpu.VMEM((rows, kw), bf), pltpu.VMEM((rows, kw), bf), dma((3,)),
             pltpu.VMEM((nr, R, wr, sub), bf),
             pltpu.VMEM((T, rows, dcols), bf),
             pltpu.VMEM((R, pr, 2 * kw), bf),

time: 140 us -> 138 us (0.986)
  no operation moved by 1% of the time
where the time goes in v3:
time: 138 us
  Pallas kernels  137 us (99%)
    pallas_call x1, Pallas kernels, body(): pl.pallas_call(functools.partial(kernel, R, T), out_shape=(jax.ShapeDtype...  133 us
    pallas_call x1, Pallas kernels, body(): pl.pallas_call(hand_out, out_shape=tuple((jax.ShapeDtypeStruct(g.shape, g...  3.87 us

profile of v3, /device:TPU:0, one launch (start us, length us, event | category | flops | bytes accessed | tf_op | source)
XLA Modules:
  0.0 138.1 jit_solution(11683080082199658687)
XLA Ops:
  1.3 132.9 %gather_project_attend.1 = (bf16[384,2048]{1,0:T(8,128)(2,1)}, bf16[384,512]{1,0:T(8,128)(2,1)}, bf16[384,512]{1,0:T(8,128)(2,1)}, f32[4,512]{1,0:T(4,128)}, f32[4,512]{1,0:T(4,128)}) custom-call(s32[1]{0:T(128)S(6)} %copy.13.len_ref, bf16[384,2560]{1,0:T(8,128)(2,1)} %g_hbm.1, bf16[320,2048]{1,0:T(8,128)(2,1)} %w_hbm.1, bf16[4,512]{1,0:T(4,128)(2,1)} %pk_hbm.1, ...), custom_call_target="tpu_custom_call" | custom-call | tf_op jit(solution)/shard_map/gather_project_attend/pallas_call | solution.py:328
  134.2 3.9 %hand_out.1 = (bf16[384,2048]{1,0:T(8,128)(2,1)}, bf16[384,512]{1,0:T(8,128)(2,1)}, bf16[384,512]{1,0:T(8,128)(2,1)}, f32[4,512]{1,0:T(4,128)}, f32[4,512]{1,0:T(4,128)}) custom-call(bf16[384,2048]{1,0:T(8,128)(2,1)} %get-tuple-element.10.refs_0_, bf16[384,512]{1,0:T(8,128)(2,1)} %get-tuple-element.11.refs_1_, bf16[384,512]{1,0:T(8,128)(2,1)} %get-tuple-element.12.refs_2_, ...), custom_call_target="tpu_custom_call" | custom-call | tf_op jit(solution)/shard_map/hand_out/pallas_call | solution.py:366
